TPU v7x, 256 devices: a whole 4x4x8 slice. The times are simulated.
256 devices in a mesh: row: 16 (over x, y), col: 16 (over z, core).
Axes of the slice: x: 4, y: 4, z: 8, core: 2. Of those that a mesh axis runs over, the one named last changes fastest.
Arguments:
- anc_inverse: float32 [10240, 10240], P('row', 'col'), may hold values from -0.0625 to 0.0625
- lower_anc: float32 [10240, 3, 384], P('col', None, 'row'), may hold values from -1.5 to 1.5
- upper_anc: float32 [10240, 3, 384], P('row', None, 'col'), may hold values from -0.75 to 0.75
- lower_edge: float32 [2, 384, 384], replicated, may hold values from -0.3125 to 0.3125
- upper_edge: float32 [2, 384, 384], replicated, may hold values from -0.3125 to 0.3125
- diag_inverse: float32 [3, 384, 384], replicated, may hold values from -6 to 6
- tile_mask: int32 [3, 80, 3], replicated, may hold values 0 or 1
Outputs:
- x_blocks: float32 [10240, 3, 384], P(('row', 'col'))
- y_blocks: float32 [16, 16, 40, 3, 384], P('col', 'row')
- z_blocks: float32 [3, 384, 384], P(None, 'row', 'col')
- cross_blocks: float32 [2, 2, 384, 384], P(None, None, 'row', 'col')
All inputs are finite; a program needn't handle non-finite values.
Results may differ from a plain program's by a relative error of at most 0.0001.
Values sent between devices are 32-bit elements; how exact they have to be, the bound alone decides.
No kernel may reach another device: no remote copies, remote signals or barrier semaphores. Data moves between devices by JAX's collectives and lax.ppermute only.
A program may use at most 128 MiB of HBM per device.

v0:
```python
import jax
import jax.numpy as jnp
from jax import lax
from jax.sharding import PartitionSpec as P

W = 384
BLK = 128
SUPER = 3
precise = lax.Precision.HIGHEST


def product(left, right):
    return jnp.dot(left, right, precision=precise, preferred_element_type=jnp.float32)


def inner_product(left, right):
    return lax.dot_general(
        left, right, (((0,), (0,)), ((), ())), precision=precise, preferred_element_type=jnp.float32
    )


def outer_product(left, right):
    return lax.dot_general(
        left, right, (((1,), (1,)), ((), ())), precision=precise, preferred_element_type=jnp.float32
    )


def tile_pattern(tile_mask, first_block, blocks):
    window = lax.dynamic_slice_in_dim(tile_mask, first_block, blocks, 1).astype(jnp.float32)
    window = jnp.transpose(window, (1, 0, 2))
    widened = jnp.broadcast_to(window[:, None, :, :, None], (blocks, BLK, SUPER, W // BLK, BLK))
    return widened.reshape(blocks * BLK, SUPER, W)


def row_term(anc_inverse, lower_cols):
    return product(anc_inverse, lower_cols)


def col_term(anc_inverse, upper_rows):
    return inner_product(anc_inverse, upper_rows)


def per_device(anc_inverse, lower_anc, upper_anc, lower_edge, upper_edge, diag_inverse, tile_mask):
    rows_here, cols_here = anc_inverse.shape
    slab_rows = rows_here // lax.axis_size("col")
    row_index = lax.axis_index("row")
    col_index = lax.axis_index("col")
    col_pattern = tile_pattern(tile_mask, col_index * (cols_here // BLK), cols_here // BLK)
    row_pattern = tile_pattern(tile_mask, row_index * (rows_here // BLK), rows_here // BLK)
    lower_list = []
    upper_list = []
    cols_list = []
    rows_list = []
    for node_index in range(SUPER):
        lower_cur = (
            lax.all_gather(lower_anc[:, node_index, :], "row", axis=1, tiled=True)
            * col_pattern[:, node_index, :]
        )
        upper_cur = (
            lax.all_gather(upper_anc[:, node_index, :], "col", axis=1, tiled=True)
            * row_pattern[:, node_index, :]
        )
        lower_list.append(lower_cur)
        upper_list.append(upper_cur)
        cols_list.append(
            lax.psum_scatter(
                row_term(anc_inverse, lower_cur), "col", scatter_dimension=0, tiled=True
            )
        )
        rows_list.append(
            lax.psum_scatter(
                col_term(anc_inverse, upper_cur), "row", scatter_dimension=0, tiled=True
            )
        )
    x_list = []
    y_list = []
    corner_list = []
    cross_cols = []
    cross_rows = []
    for node_index in range(SUPER):
        lower_cur = lower_list[node_index]
        upper_cur = upper_list[node_index]
        inv_cols = -cols_list[node_index]
        inv_rows = -rows_list[node_index]
        upper_mine = lax.dynamic_slice_in_dim(upper_cur, col_index * slab_rows, slab_rows, 0)
        if node_index > 0:
            lower_side = lower_edge[node_index - 1]
            upper_side = upper_edge[node_index - 1]
            lower_mine = lax.dynamic_slice_in_dim(lower_cur, row_index * slab_rows, slab_rows, 0)
            rows_lower = inner_product(prev_rows, lower_mine)
            upper_cols = inner_product(upper_mine, prev_cols)
        if node_index > 0:
            rows_lower, upper_cols = lax.psum((rows_lower, upper_cols), ("row", "col"))
        if node_index > 0:
            cross_col = -(rows_lower + product(prev_corner, lower_side))
            cross_row = -(upper_cols + product(upper_side, prev_corner))
            inv_cols = inv_cols - product(prev_cols, lower_side)
            inv_rows = inv_rows - outer_product(prev_rows, upper_side)
            cross_cols.append(cross_col)
            cross_rows.append(cross_row)
        inv_corner = diag_inverse[node_index] - lax.psum(
            inner_product(upper_mine, inv_cols), ("row", "col")
        )
        if node_index > 0:
            inv_corner = inv_corner - product(upper_side, cross_col)
        x_list.append(inv_cols)
        y_list.append(inv_rows)
        corner_list.append(inv_corner)
        prev_cols = inv_cols
        prev_rows = inv_rows
        prev_corner = inv_corner
    x_blocks = jnp.stack(x_list, axis=1)
    y_blocks = jnp.stack(y_list, axis=1)[None, None]
    tile_rows = W // lax.axis_size("row")
    tile_cols = W // lax.axis_size("col")
    corners = jnp.stack(corner_list)
    corners = lax.dynamic_slice_in_dim(corners, row_index * tile_rows, tile_rows, 1)
    z_blocks = lax.dynamic_slice_in_dim(corners, col_index * tile_cols, tile_cols, 2)
    crossed = jnp.stack([jnp.stack(cross_cols), jnp.stack(cross_rows)])
    crossed = lax.dynamic_slice_in_dim(crossed, row_index * tile_rows, tile_rows, 2)
    cross_blocks = lax.dynamic_slice_in_dim(crossed, col_index * tile_cols, tile_cols, 3)
    return (x_blocks, y_blocks, z_blocks, cross_blocks)


def solution(mesh):
    return jax.shard_map(
        per_device,
        mesh=mesh,
        in_specs=(
            P("row", "col"),
            P("col", None, "row"),
            P("row", None, "col"),
            P(),
            P(),
            P(),
            P(),
        ),
        out_specs=(
            P(("row", "col"), None, None),
            P("col", "row", None, None, None),
            P(None, "row", "col"),
            P(None, None, "row", "col"),
        ),
        check_vma=False,
    )
```

profile of v0, /device:TPU:4, one launch (start us, length us, event | category | flops | bytes accessed | tf_op | source)
XLA Modules:
  0.0 653.5 jit_solution(15798240488232442538)
XLA Ops:
  8.3 26.5 %all-gather = f32[640,1,384]{0,1,2:T(1,128)} all-gather(f32[640,1,24]{0,1,2:T(1,128)S(1)} %copy.79), channel_id=2, replica_groups=mesh['row'=16,'col'=16] {'row'}, dimensions={2}, use_global_device_ids=true | all-gather | bytes 1044480 | tf_op jit(solution)/shard_map/all_gather | solution.py:56
  39.8 5.9 reshape.16
  45.7 24.7 %all-gather.2 = f32[640,1,384]{0,1,2:T(1,128)} all-gather(f32[640,1,24]{0,1,2:T(1,128)S(1)} %copy.81), channel_id=4, replica_groups=mesh['row'=16,'col'=16] {'row'}, dimensions={2}, use_global_device_ids=true | all-gather | bytes 1044480 | tf_op jit(solution)/shard_map/all_gather | solution.py:56
  70.5 3.2 copy.46
  73.8 25.1 %all-gather.1 = f32[640,1,384]{0,1,2:T(1,128)} all-gather(f32[640,1,24]{0,1,2:T(1,128)S(1)} %copy.80), channel_id=3, replica_groups=mesh['row'=16,'col'=16] {'row'}, dimensions={2}, use_global_device_ids=true | all-gather | bytes 1044480 | tf_op jit(solution)/shard_map/all_gather | solution.py:56
  98.9 3.7 copy.43
  102.7 7.1 %convolution_bitcast_fusion.5 = f32[640,384]{0,1:T(8,128)} fusion(f32[640,640]{1,0:T(8,128)S(1)} %copy-done, f32[640,1,384]{2,0,1:T(8,128)S(1)} %copy.41, f32[640,3,384]{2,0,1:T(8,128)} %reshape.16), kind=kOutput, calls=%fused_computation.10 | convolution fusion | flops 1887682560 | bytes 4587520 | tf_op jit(solution)/shard_map/dot_general | solution.py:13
  111.3 5.9 convolution_bitcast_fusion.4
  117.2 6.1 convolution_bitcast_fusion.3
  124.3 24.7 %all-gather.5 = f32[640,1,384]{0,1,2:T(1,128)} all-gather(f32[640,1,24]{0,1,2:T(1,128)S(1)} %copy.84), channel_id=7, replica_groups=mesh['row'=16,'col'=16] {'col'}, dimensions={2}, use_global_device_ids=true | all-gather | bytes 1044480 | tf_op jit(solution)/shard_map/all_gather | solution.py:60
  149.1 18.5 %all-gather.4 = f32[640,1,384]{0,1,2:T(1,128)S(1)} all-gather(f32[640,1,24]{0,1,2:T(1,128)S(1)} %copy.83), channel_id=6, replica_groups=mesh['row'=16,'col'=16] {'col'}, dimensions={2}, use_global_device_ids=true | all-gather | bytes 1044480 | tf_op jit(solution)/shard_map/all_gather | solution.py:60
  167.6 21.5 %all-gather.3 = f32[640,1,384]{0,1,2:T(1,128)} all-gather(f32[640,1,24]{0,1,2:T(1,128)S(1)} %copy.82), channel_id=5, replica_groups=mesh['row'=16,'col'=16] {'col'}, dimensions={2}, use_global_device_ids=true | all-gather | bytes 1044480 | tf_op jit(solution)/shard_map/all_gather | solution.py:60
  189.1 3.2 copy.56
  194.9 5.9 reshape.17
  202.7 3.3 copy.51
  206.0 2.7 slice_multiply_fusion
  208.8 3.9 convolution_bitcast_fusion.2
  212.7 3.9 convolution_bitcast_fusion.1
  216.6 3.9 convolution_bitcast_fusion
  223.7 21.6 %all-reduce.15.cloned.1.call-done = (f32[640,384]{0,1:T(8,128)}, f32[640,384]{0,1:T(8,128)}, f32[640,384]{0,1:T(8,128)}) async-done(((f32[640,384]{0,1:T(8,128)}, f32[640,384]{0,1:T(8,128)}, f32[640,384]{0,1:T(8,128)}), (f32[640,384]{0,1:T(8,128)}, f32[640,384]{0,1:T(8,128)}, f32[640,384]{0,1:T(8,128)})) %all-reduce.15.cloned.1.call-update) | async-done | bytes 2949136
  246.8 2.8 fusion.42
  249.6 2.9 fusion.41
  261.6 91.4 %all-reduce.17.cloned.1.call-done = (f32[640,384]{0,1:T(8,128)}, f32[640,384]{0,1:T(8,128)}, f32[640,384]{0,1:T(8,128)}) async-done(((f32[640,384]{0,1:T(8,128)}, f32[640,384]{0,1:T(8,128)}, f32[640,384]{0,1:T(8,128)}), (f32[640,384]{0,1:T(8,128)}, f32[640,384]{0,1:T(8,128)}, f32[640,384]{0,1:T(8,128)})) %all-reduce.17.cloned.1.call-update) | async-done | bytes 2949136
  366.8 267.0 %all-reduce.13.cloned.1.call-done = (f32[384,384]{1,0:T(8,128)}, f32[384,384]{1,0:T(8,128)}, f32[384,384]{1,0:T(8,128)}, f32[384,384]{1,0:T(8,128)}, f32[384,384...) async-done(((f32[384,384]{1,0:T(8,128)}, f32[384,384]{1,0:T(8,128)}, f32[384,384]{1,0:T(8,128)}, f32[384,384]{1,0:T(8,128)}, f32[384,384]{1,0:T(8,128)}, ...) | async-done | bytes 4128784 | tf_op jit(solution)/shard_map/psum | solution.py:93
  (105 shorter events, 52.1 us)
Async XLA Ops:
  7.2 95.5 %copy-start = (f32[640,640]{1,0:T(8,128)S(1)}, f32[640,640]{1,0:T(8,128)}, u32[]{:S(2)}) copy-start(f32[640,640]{1,0:T(8,128)} %param.7) | copy-start | bytes 4915204
  7.2 238.1 %all-reduce.15.cloned.1.call-start = ((), (), s32[]{:S(2)}) async-start(), calls=%async_computation.1 | async-start | bytes 5898240
  8.2 28.9 %copy-start.21 = (s32[3,80,3]{1,2,0:T(4,128)S(1)}, s32[3,80,3]{1,2,0:T(4,128)}, u32[]{:S(2)}) copy-start(s32[3,80,3]{1,2,0:T(4,128)} %param.13) | copy-start | bytes 8644
  102.7 7.1 %copy-start.1 = (f32[640,3,384]{2,0,1:T(8,128)S(1)}, f32[640,3,384]{2,0,1:T(8,128)}, u32[]{:S(2)}) copy-start(f32[640,3,384]{2,0,1:T(8,128)} %reshape.16) | copy-start | bytes 8847364
  102.7 7.1 %copy-start.14 = (f32[640,1,384]{2,0,1:T(8,128)S(1)}, f32[640,1,384]{2,0,1:T(8,128)}, u32[]{:S(2)}) copy-start(f32[640,1,384]{2,0,1:T(8,128)} %copy.46) | copy-start | bytes 2949124
  111.3 5.9 copy-start.11
  111.3 5.9 copy-start.10
  123.3 229.7 %all-reduce.17.cloned.1.call-start = ((), (), s32[]{:S(2)}) async-start(), calls=%async_computation.2 | async-start | bytes 5898240
  202.7 3.3 copy-start.13
  208.7 3.9 copy-start.12
  208.7 3.9 copy-start.9
  208.7 7.9 %copy-start.8 = (f32[640,1,384]{2,0,1:T(8,128)}, f32[640,1,384]{2,0,1:T(8,128)S(1)}, u32[]{:S(2)}) copy-start(f32[640,1,384]{2,0,1:T(8,128)S(1)} %get-tuple-element.25) | copy-start | bytes 2949124
  220.6 32.0 %copy-start.5 = (f32[2,384,384]{2,1,0:T(8,128)S(1)}, f32[2,384,384]{2,1,0:T(8,128)}, u32[]{:S(2)}) copy-start(f32[2,384,384]{2,1,0:T(8,128)} %param.10) | copy-start | bytes 3538948
  220.6 413.2 %all-reduce.13.cloned.1.call-start = ((), (), s32[]{:S(2)}) async-start(), calls=%async_computation | async-start | bytes 8257536 | tf_op jit(solution)/shard_map/psum | solution.py:93
  249.6 9.2 %copy-start.6 = (f32[2,384,384]{2,1,0:T(8,128)S(1)}, f32[2,384,384]{2,1,0:T(8,128)}, u32[]{:S(2)}) copy-start(f32[2,384,384]{2,1,0:T(8,128)} %param.10) | copy-start | bytes 3538948
  258.8 97.9 %copy-start.2 = (f32[2,384,384]{2,1,0:T(8,128)S(1)}, f32[2,384,384]{2,1,0:T(8,128)}, u32[]{:S(2)}) copy-start(f32[2,384,384]{2,1,0:T(8,128)} %param.11) | copy-start | bytes 3538948
  633.8 1.5 copy-start.3
  633.8 1.8 copy-start.7
  635.2 3.1 copy-start.4
  635.2 3.1 copy-start.19
  638.3 1.3 copy-start.18
  639.6 1.3 copy-start.17
  640.9 1.6 copy-start.16
  642.5 1.3 copy-start.15
  (3 other events, 2.9 us)
Sparse Core Ops, SparseCore 0:
  123.5 121.7 all-reduce.14
  249.0 103.9 all-reduce.16
  361.1 272.6 all-reduce.12
where the time goes:
time: 658 us; the launch traced here: 653 us
  waiting for transfers between devices  380 us (58%)
  blocking collectives  141 us (21%)
  matrix products  62.5 us (9%)
  local copies, waits for them, and re-layouts  42.9 us (7%)
  between operations  15.7 us (2%)
  other arithmetic  10.9 us (2%)
    psum x1, waiting for transfers between devices, per_device(): rows_lower, upper_cols = lax.psum((rows_lower, upper_cols), ('row', 'col'))  267 us
    unnamed x5, waiting for transfers between devices  113 us
    all_gather x3, blocking collectives, per_device(): lax.all_gather(lower_anc[:, node_index, :], 'row', axis=1, tiled=True)  76.4 us
    all_gather x3, blocking collectives, per_device(): lax.all_gather(upper_anc[:, node_index, :], 'col', axis=1, tiled=True)  64.6 us
    dot_general x11, matrix products, product(): jnp.dot(left, right, precision=precise, preferred_element_type=jnp.float32)  30.5 us
    dot_general x10, matrix products, inner_product(): lax.dot_general(left, right, (((0,), (0,)), ((), ())), precision=precise,...  29.4 us
  transfers between devices with their start and end apart: 3, of which 3 were waited for; matrix products, arithmetic and copies ran while one was open for 8% of the time, Pallas kernels for 0%

commit v1 on v0

--- a/solution.py
+++ b/solution.py
@@ -7,6 +7,24 @@
 BLK = 128
 SUPER = 3
 precise = lax.Precision.HIGHEST
+
+
+def ring_gather(array, axis, dim):
+    ways, here, step = (lax.axis_size(axis), lax.axis_index(axis), array.shape[dim])
+    shape = [n * ways if d == dim else n for d, n in enumerate(array.shape)]
+    full = lax.dynamic_update_slice_in_dim(
+        jnp.zeros(shape, array.dtype), array, here * step, axis=dim
+    )
+    going_up = going_down = array
+    for far in range(1, ways // 2 + 1):
+        going_up = lax.ppermute(going_up, axis, [(d, (d + 1) % ways) for d in range(ways)])
+        full = lax.dynamic_update_slice_in_dim(full, going_up, (here - far) % ways * step, axis=dim)
+        if 2 * far < ways:
+            going_down = lax.ppermute(going_down, axis, [(d, (d - 1) % ways) for d in range(ways)])
+            full = lax.dynamic_update_slice_in_dim(
+                full, going_down, (here + far) % ways * step, axis=dim
+            )
+    return full
 
 
 def product(left, right):
@@ -57,8 +75,7 @@
             * col_pattern[:, node_index, :]
         )
         upper_cur = (
-            lax.all_gather(upper_anc[:, node_index, :], "col", axis=1, tiled=True)
-            * row_pattern[:, node_index, :]
+            ring_gather(upper_anc[:, node_index, :], "col", 1) * row_pattern[:, node_index, :]
         )
         lower_list.append(lower_cur)
         upper_list.append(upper_cur)

time: 658 us -> 818 us (1.24)
  local copies, waits for them, and re-layouts: 42.9 us -> 222 us
  blocking collectives: 141 us -> 75.2 us
  starting transfers between devices: 0.33 us -> 59.2 us
  waiting for transfers between devices: 380 us -> 360 us
    dynamic_update_slice x0 -> x48, local copies, waits for them, and re-layouts: none -> 183 us  [the longest x24 87.1 us: ring_gather(): lax.dynamic_update_slice_in_dim(full, going_up, (here - far) % ways * ste...]
    all_gather x3 -> x0, blocking collectives: 64.6 us -> none  [per_device(): lax.all_gather(upper_anc[:, node_index, :], 'col', axis=1, tiled=True)]
    ppermute x0 -> x45, starting transfers between devices: none -> 58.8 us  [the longest x21 58.2 us: ring_gather(): lax.ppermute(going_down, axis, [(d, (d - 1) % ways) for d in range(ways)])]
    unnamed x5, waiting for transfers between devices: 113 us -> 83.2 us
    ppermute x0 -> x45, waiting for transfers between devices: none -> 10.1 us  [the longest x24 7.2 us: ring_gather(): lax.ppermute(going_up, axis, [(d, (d + 1) % ways) for d in range(ways)])]
    all_gather x3 -> x0, local copies, waits for them, and re-layouts: 8.47 us -> none  [per_device(): lax.all_gather(upper_anc[:, node_index, :], 'col', axis=1, tiled=True)]
  transfers between devices with their start and end apart: 3 -> 48, of which waited for: 3 -> 6; matrix products, arithmetic and copies ran while one was open for 8% -> 34% of each run, Pallas kernels for 0% -> 0%
where the time goes in v1:
time: 818 us; the launch traced here: 808 us
  waiting for transfers between devices  360 us (44%)
  local copies, waits for them, and re-layouts  222 us (27%)
  blocking collectives  75.2 us (9%)
  matrix products  62.4 us (8%)
  starting transfers between devices  59.2 us (7%)
  between operations  16.4 us (2%)
  other arithmetic  12.6 us (2%)
    psum x1, waiting for transfers between devices, per_device(): rows_lower, upper_cols = lax.psum((rows_lower, upper_cols), ('row', 'col'))  267 us
    dynamic_update_slice x24, local copies, waits for them, and re-layouts, ring_gather(): lax.dynamic_update_slice_in_dim(full, going_up, (here - far) % ways * ste...  87.1 us
    dynamic_update_slice x21, local copies, waits for them, and re-layouts, ring_gather(): lax.dynamic_update_slice_in_dim(full, going_down, (here + far) % ways * s...  85 us
    unnamed x5, waiting for transfers between devices  83.2 us
    all_gather x3, blocking collectives, per_device(): lax.all_gather(lower_anc[:, node_index, :], 'row', axis=1, tiled=True)  75.2 us
    ppermute x21, starting transfers between devices, ring_gather(): lax.ppermute(going_down, axis, [(d, (d - 1) % ways) for d in range(ways)])  58.2 us
    dot_general x11, matrix products, product(): jnp.dot(left, right, precision=precise, preferred_element_type=jnp.float32)  30.6 us
    dot_general x10, matrix products, inner_product(): lax.dot_general(left, right, (((0,), (0,)), ((), ())), precision=precise,...  29.3 us
  transfers between devices with their start and end apart: 48, of which 6 were waited for; matrix products, arithmetic and copies ran while one was open for 34% of the time, Pallas kernels for 0%

profile of v1, /device:TPU:4, one launch (start us, length us, event | category | flops | bytes accessed | tf_op | source)
XLA Modules:
  0.0 807.8 jit_solution(14514764023088938508)
XLA Ops:
  8.5 5.3 collective-permute-start.1
  17.9 24.7 %all-gather.1 = f32[640,1,384]{0,1,2:T(1,128)S(1)} all-gather(f32[640,1,24]{0,1,2:T(1,128)S(1)} %copy.77), channel_id=3, replica_groups=mesh['row'=16,'col'=16] {'row'}, dimensions={2}, use_global_device_ids=true | all-gather | bytes 1044480 | tf_op jit(solution)/shard_map/all_gather | solution.py:74
  42.8 25.0 %all-gather.2 = f32[640,1,384]{0,1,2:T(1,128)} all-gather(f32[640,1,24]{0,1,2:T(1,128)S(1)} %copy.78), channel_id=4, replica_groups=mesh['row'=16,'col'=16] {'row'}, dimensions={2}, use_global_device_ids=true | all-gather | bytes 1044480 | tf_op jit(solution)/shard_map/all_gather | solution.py:74
  76.4 5.9 reshape.16
  105.6 25.4 %all-gather = f32[640,1,384]{0,1,2:T(1,128)} all-gather(f32[640,1,24]{0,1,2:T(1,128)S(1)} %copy.76), channel_id=2, replica_groups=mesh['row'=16,'col'=16] {'row'}, dimensions={2}, use_global_device_ids=true | all-gather | bytes 1044480 | tf_op jit(solution)/shard_map/all_gather | solution.py:74
  140.4 7.3 convolution_bitcast_fusion.5
  156.6 5.8 convolution_bitcast_fusion.3
  169.0 6.3 convolution_bitcast_fusion.4
  192.0 4.3 collective-permute-done.42
  211.3 5.9 reshape.17
  235.0 4.4 dynamic_update_slice.178
  257.3 4.4 dynamic_update_slice.180
  279.6 4.4 dynamic_update_slice.182
  301.7 4.8 dynamic_update_slice.184
  324.5 4.7 dynamic_update_slice.186
  344.4 4.4 dynamic_update_slice.187
  348.8 4.4 dynamic_update_slice.188
  360.9 4.4 dynamic_update_slice.189
  372.8 4.4 dynamic_update_slice.190
  384.9 4.6 dynamic_update_slice.191
  392.2 3.9 convolution_bitcast_fusion
  396.1 3.9 convolution_bitcast_fusion.1
  423.4 83.2 %all-reduce.17.cloned.1.call-done = (f32[640,384]{0,1:T(8,128)}, f32[640,384]{0,1:T(8,128)}, f32[640,384]{0,1:T(8,128)}) async-done(((f32[640,384]{0,1:T(8,128)}, f32[640,384]{0,1:T(8,128)}, f32[640,384]{0,1:T(8,128)}), (f32[640,384]{0,1:T(8,128)}, f32[640,384]{0,1:T(8,128)}, f32[640,384]{0,1:T(8,128)})) %all-reduce.17.cloned.1.call-update) | async-done | bytes 2949136
  520.3 267.0 %all-reduce.13.cloned.1.call-done = (f32[384,384]{1,0:T(8,128)}, f32[384,384]{1,0:T(8,128)}, f32[384,384]{1,0:T(8,128)}, f32[384,384]{1,0:T(8,128)}, f32[384,384...) async-done(((f32[384,384]{1,0:T(8,128)}, f32[384,384]{1,0:T(8,128)}, f32[384,384]{1,0:T(8,128)}, f32[384,384]{1,0:T(8,128)}, f32[384,384]{1,0:T(8,128)}, ...) | async-done | bytes 4128784 | tf_op jit(solution)/shard_map/psum | solution.py:110
  (268 shorter events, 272.8 us)
Async XLA Ops:
  7.2 399.9 %all-reduce.15.cloned.1.call-start = ((), (), s32[]{:S(2)}) async-start(), calls=%async_computation.1 | async-start | bytes 5898240
  8.5 59.3 %collective-permute-start = (f32[640,24]{1,0:T(8,128)S(1)}, f32[640,24]{1,0:T(8,128)}, u32[]{:S(2)}, u32[]{:S(2)}) collective-permute-start(f32[640,24]{1,0:T(8,128)S(1)} %bitcast.175), channel_id=1, source_target_pairs={{0,1},{1,2},{2,3},{3,4},{4,5},{5,6},{6,7},{7,8},{8,9},{9,10},{10,1... | collective-permute-start | bytes 184328 | tf_op jit(solution)/shard_map/ppermute | solution.py:20
  8.5 59.3 %collective-permute-start.1 = (f32[640,24]{1,0:T(8,128)S(1)}, f32[640,24]{1,0:T(8,128)}, u32[]{:S(2)}, u32[]{:S(2)}) collective-permute-start(f32[640,24]{1,0:T(8,128)S(1)} %bitcast.176), channel_id=1, source_target_pairs={{0,15},{1,0},{2,1},{3,2},{4,3},{5,4},{6,5},{7,6},{8,7},{9,8},{10,9... | collective-permute-start | bytes 184328 | tf_op jit(solution)/shard_map/ppermute | solution.py:23
  14.0 54.3 %collective-permute-start.15 = (f32[640,24]{1,0:T(8,128)S(1)}, f32[640,24]{1,0:T(8,128)}, u32[]{:S(2)}, u32[]{:S(2)}) collective-permute-start(f32[640,24]{1,0:T(8,128)S(1)} %bitcast.178), channel_id=1, source_target_pairs={{0,1},{1,2},{2,3},{3,4},{4,5},{5,6},{6,7},{7,8},{8,9},{9,10},{10,1... | collective-permute-start | bytes 184328 | tf_op jit(solution)/shard_map/ppermute | solution.py:20
  14.0 56.8 %collective-permute-start.16 = (f32[640,24]{1,0:T(8,128)S(1)}, f32[640,24]{1,0:T(8,128)}, u32[]{:S(2)}, u32[]{:S(2)}) collective-permute-start(f32[640,24]{1,0:T(8,128)S(1)} %bitcast.179), channel_id=1, source_target_pairs={{0,15},{1,0},{2,1},{3,2},{4,3},{5,4},{6,5},{7,6},{8,7},{9,8},{10,9... | collective-permute-start | bytes 184328 | tf_op jit(solution)/shard_map/ppermute | solution.py:23
  17.9 53.0 %collective-permute-start.30 = (f32[640,24]{1,0:T(8,128)}, f32[640,24]{1,0:T(8,128)}, u32[]{:S(2)}, u32[]{:S(2)}) collective-permute-start(f32[640,24]{1,0:T(8,128)} %bitcast.22), channel_id=1, source_target_pairs={{0,1},{1,2},{2,3},{3,4},{4,5},{5,6},{6,7},{7,8},{8,9},{9,10},{10,1... | collective-permute-start | bytes 184328 | tf_op jit(solution)/shard_map/ppermute | solution.py:20
  67.8 19.6 %collective-permute-start.31 = (f32[640,24]{1,0:T(8,128)}, f32[640,24]{1,0:T(8,128)}, u32[]{:S(2)}, u32[]{:S(2)}) collective-permute-start(f32[640,24]{1,0:T(8,128)} %bitcast.22), channel_id=1, source_target_pairs={{0,15},{1,0},{2,1},{3,2},{4,3},{5,4},{6,5},{7,6},{8,7},{9,8},{10,9... | collective-permute-start | bytes 184328 | tf_op jit(solution)/shard_map/ppermute | solution.py:23
  67.8 19.6 %collective-permute-start.2 = (f32[640,24]{1,0:T(8,128)}, f32[640,24]{1,0:T(8,128)}, u32[]{:S(2)}, u32[]{:S(2)}) collective-permute-start(f32[640,24]{1,0:T(8,128)} %collective-permute-done), channel_id=1, source_target_pairs={{0,1},{1,2},{2,3},{3,4},{4,5},{5,6},{6,7},{7,8},{8,9},{9,10},{10,1... | collective-permute-start | bytes 184328 | tf_op jit(solution)/shard_map/ppermute | solution.py:20
  68.3 22.1 %collective-permute-start.3 = (f32[640,24]{1,0:T(8,128)}, f32[640,24]{1,0:T(8,128)}, u32[]{:S(2)}, u32[]{:S(2)}) collective-permute-start(f32[640,24]{1,0:T(8,128)} %collective-permute-done.1), channel_id=1, source_target_pairs={{0,15},{1,0},{2,1},{3,2},{4,3},{5,4},{6,5},{7,6},{8,7},{9,8},{10,9... | collective-permute-start | bytes 184328 | tf_op jit(solution)/shard_map/ppermute | solution.py:23
  70.8 19.6 %collective-permute-start.17 = (f32[640,24]{1,0:T(8,128)}, f32[640,24]{1,0:T(8,128)}, u32[]{:S(2)}, u32[]{:S(2)}) collective-permute-start(f32[640,24]{1,0:T(8,128)} %collective-permute-done.15), channel_id=1, source_target_pairs={{0,1},{1,2},{2,3},{3,4},{4,5},{5,6},{6,7},{7,8},{8,9},{9,10},{10,1... | collective-permute-start | bytes 184328 | tf_op jit(solution)/shard_map/ppermute | solution.py:20
  70.8 22.6 %collective-permute-start.18 = (f32[640,24]{1,0:T(8,128)}, f32[640,24]{1,0:T(8,128)}, u32[]{:S(2)}, u32[]{:S(2)}) collective-permute-start(f32[640,24]{1,0:T(8,128)} %collective-permute-done.16), channel_id=1, source_target_pairs={{0,15},{1,0},{2,1},{3,2},{4,3},{5,4},{6,5},{7,6},{8,7},{9,8},{10,9... | collective-permute-start | bytes 184328 | tf_op jit(solution)/shard_map/ppermute | solution.py:23
  96.7 37.8 %collective-permute-start.20 = (f32[640,24]{1,0:T(8,128)}, f32[640,24]{1,0:T(8,128)}, u32[]{:S(2)}, u32[]{:S(2)}) collective-permute-start(f32[640,24]{1,0:T(8,128)} %collective-permute-done.18), channel_id=1, source_target_pairs={{0,15},{1,0},{2,1},{3,2},{4,3},{5,4},{6,5},{7,6},{8,7},{9,8},{10,9... | collective-permute-start | bytes 184328 | tf_op jit(solution)/shard_map/ppermute | solution.py:23
  99.6 34.8 %collective-permute-start.34 = (f32[640,24]{1,0:T(8,128)}, f32[640,24]{1,0:T(8,128)}, u32[]{:S(2)}, u32[]{:S(2)}) collective-permute-start(f32[640,24]{1,0:T(8,128)} %collective-permute-done.32), channel_id=1, source_target_pairs={{0,1},{1,2},{2,3},{3,4},{4,5},{5,6},{6,7},{7,8},{8,9},{9,10},{10,1... | collective-permute-start | bytes 184328 | tf_op jit(solution)/shard_map/ppermute | solution.py:20
  99.6 37.8 %collective-permute-start.35 = (f32[640,24]{1,0:T(8,128)}, f32[640,24]{1,0:T(8,128)}, u32[]{:S(2)}, u32[]{:S(2)}) collective-permute-start(f32[640,24]{1,0:T(8,128)} %collective-permute-done.33), channel_id=1, source_target_pairs={{0,15},{1,0},{2,1},{3,2},{4,3},{5,4},{6,5},{7,6},{8,7},{9,8},{10,9... | collective-permute-start | bytes 184328 | tf_op jit(solution)/shard_map/ppermute | solution.py:23
  102.6 34.8 %collective-permute-start.6 = (f32[640,24]{1,0:T(8,128)}, f32[640,24]{1,0:T(8,128)}, u32[]{:S(2)}, u32[]{:S(2)}) collective-permute-start(f32[640,24]{1,0:T(8,128)} %collective-permute-done.4), channel_id=1, source_target_pairs={{0,1},{1,2},{2,3},{3,4},{4,5},{5,6},{6,7},{7,8},{8,9},{9,10},{10,1... | collective-permute-start | bytes 184328 | tf_op jit(solution)/shard_map/ppermute | solution.py:20
  102.6 37.8 %collective-permute-start.7 = (f32[640,24]{1,0:T(8,128)}, f32[640,24]{1,0:T(8,128)}, u32[]{:S(2)}, u32[]{:S(2)}) collective-permute-start(f32[640,24]{1,0:T(8,128)} %collective-permute-done.5), channel_id=1, source_target_pairs={{0,15},{1,0},{2,1},{3,2},{4,3},{5,4},{6,5},{7,6},{8,7},{9,8},{10,9... | collective-permute-start | bytes 184328 | tf_op jit(solution)/shard_map/ppermute | solution.py:23
  165.3 16.9 %collective-permute-start.26 = (f32[640,24]{1,0:T(8,128)}, f32[640,24]{1,0:T(8,128)}, u32[]{:S(2)}, u32[]{:S(2)}) collective-permute-start(f32[640,24]{1,0:T(8,128)} %collective-permute-done.24), channel_id=1, source_target_pairs={{0,15},{1,0},{2,1},{3,2},{4,3},{5,4},{6,5},{7,6},{8,7},{9,8},{10,9... | collective-permute-start | bytes 184328 | tf_op jit(solution)/shard_map/ppermute | solution.py:23
  175.4 331.2 %all-reduce.17.cloned.1.call-start = ((), (), s32[]{:S(2)}) async-start(), calls=%async_computation.2 | async-start | bytes 5898240
  183.8 185.1 %collective-permute-start.28 = (f32[640,24]{1,0:T(8,128)}, f32[640,24]{1,0:T(8,128)}, u32[]{:S(2)}, u32[]{:S(2)}) collective-permute-start(f32[640,24]{1,0:T(8,128)} %collective-permute-done.26), channel_id=1, source_target_pairs={{0,15},{1,0},{2,1},{3,2},{4,3},{5,4},{6,5},{7,6},{8,7},{9,8},{10,9... | collective-permute-start | bytes 184328 | tf_op jit(solution)/shard_map/ppermute | solution.py:23
  187.1 185.7 %collective-permute-start.43 = (f32[640,24]{1,0:T(8,128)}, f32[640,24]{1,0:T(8,128)}, u32[]{:S(2)}, u32[]{:S(2)}) collective-permute-start(f32[640,24]{1,0:T(8,128)} %collective-permute-done.41), channel_id=1, source_target_pairs={{0,15},{1,0},{2,1},{3,2},{4,3},{5,4},{6,5},{7,6},{8,7},{9,8},{10,9... | collective-permute-start | bytes 184328 | tf_op jit(solution)/shard_map/ppermute | solution.py:23
  189.2 188.1 %collective-permute-start.14 = (f32[640,24]{1,0:T(8,128)}, f32[640,24]{1,0:T(8,128)}, u32[]{:S(2)}, u32[]{:S(2)}) collective-permute-start(f32[640,24]{1,0:T(8,128)} %collective-permute-done.12), channel_id=1, source_target_pairs={{0,1},{1,2},{2,3},{3,4},{4,5},{5,6},{6,7},{7,8},{8,9},{9,10},{10,1... | collective-permute-start | bytes 184328 | tf_op jit(solution)/shard_map/ppermute | solution.py:20
  192.0 189.1 %collective-permute-start.29 = (f32[640,24]{1,0:T(8,128)}, f32[640,24]{1,0:T(8,128)}, u32[]{:S(2)}, u32[]{:S(2)}) collective-permute-start(f32[640,24]{1,0:T(8,128)} %collective-permute-done.27), channel_id=1, source_target_pairs={{0,1},{1,2},{2,3},{3,4},{4,5},{5,6},{6,7},{7,8},{8,9},{9,10},{10,1... | collective-permute-start | bytes 184328 | tf_op jit(solution)/shard_map/ppermute | solution.py:20
  196.3 188.6 %collective-permute-start.44 = (f32[640,24]{1,0:T(8,128)}, f32[640,24]{1,0:T(8,128)}, u32[]{:S(2)}, u32[]{:S(2)}) collective-permute-start(f32[640,24]{1,0:T(8,128)} %collective-permute-done.42), channel_id=1, source_target_pairs={{0,1},{1,2},{2,3},{3,4},{4,5},{5,6},{6,7},{7,8},{8,9},{9,10},{10,1... | collective-permute-start | bytes 184328 | tf_op jit(solution)/shard_map/ppermute | solution.py:20
  404.0 383.3 %all-reduce.13.cloned.1.call-start = ((), (), s32[]{:S(2)}) async-start(), calls=%async_computation | async-start | bytes 8257536 | tf_op jit(solution)/shard_map/psum | solution.py:110
  (62 other events, 912.4 us)
Sparse Core Ops, SparseCore 0:
  175.5 119.2 all-reduce.14
  404.1 102.4 all-reduce.16
  514.6 272.6 all-reduce.12
